TPU v7x, 32 devices: a whole 2x2x4 slice. The times are simulated.
32 devices in a mesh: blk: 8 (over z, y), rep: 4 (over x, core).
Axes of the slice: x: 2, y: 2, z: 4, core: 2. Of those that a mesh axis runs over, the one named last changes fastest.
Arguments:
- embeddings: bfloat16 [1024, 256], P('blk'), may hold values from -21 to 21
- targets: float32 [128, 1024], P('rep', 'blk'), may hold values from -180 to 180
Outputs:
- solution: float32 [128, 1024], P('rep', 'blk')
- residual: float32 [128, 1024], P('rep', 'blk')
All inputs are finite; a program needn't handle non-finite values.
Results may differ from a plain program's by a relative error of at most 0.0003.
Values may be sent and summed in bfloat16 or wider, within the bound.
A program may use at most 64 MiB of HBM per device.

v0:
```python
import jax
import jax.numpy as jnp
from jax import lax
from jax.sharding import PartitionSpec as P

ITERS = 2


length_scale = 1.0
noise_var = 1.0


def squared_norms(points):
    widened = points.astype(jnp.float32)
    return jnp.sum(widened * widened, axis=1)


def kernel_tile(own_points, own_norms, own_labels, far_points, far_norms, far_labels):
    products = jnp.einsum("pd,qd->pq", own_points, far_points, preferred_element_type=jnp.float32)
    distance_sq = own_norms[:, None] + far_norms[None, :] - 2.0 * products
    distance_sq = jnp.where(own_labels[:, None] == far_labels[None, :], 0.0, distance_sq)
    return jnp.exp(-jnp.sqrt(distance_sq) / length_scale)


def paired(residual, image):
    return lax.psum((jnp.sum(residual * residual), jnp.sum(residual * image)), ("blk", "rep"))


def per_device(embeddings, targets):
    block_id = lax.axis_index("blk")
    local_count = embeddings.shape[0]
    own_norms = squared_norms(embeddings)
    own_labels = block_id * local_count + jnp.arange(local_count, dtype=jnp.int32)
    everyone = lax.all_gather(embeddings, "blk", axis=0, tiled=True)
    every_norms = squared_norms(everyone)

    def folded_image(direction):
        piece = lax.all_gather(direction, "blk", axis=1, tiled=True)
        count = piece.shape[1]
        far_labels = jnp.arange(count, dtype=jnp.int32)
        tile = kernel_tile(embeddings, own_norms, own_labels, everyone, every_norms, far_labels)
        total = jnp.einsum(
            "rq,pq->rp",
            piece,
            tile,
            precision=lax.Precision.HIGHEST,
            preferred_element_type=jnp.float32,
        )
        return total + noise_var * direction

    solution = jnp.zeros_like(targets)
    residual = targets
    image = folded_image(residual)
    norm_now, product = paired(residual, image)
    alpha = norm_now / product
    direction = residual
    along = image
    for iteration in range(ITERS):
        solution = solution + alpha * direction
        residual = residual - alpha * along
        if iteration + 1 < ITERS:
            image = folded_image(residual)
            norm_next, product = paired(residual, image)
            ratio = norm_next / norm_now
            alpha = norm_next / (product - ratio * norm_next / alpha)
            direction = residual + ratio * direction
            along = image + ratio * along
            norm_now = norm_next
    return (solution, residual)


def solution(mesh):
    in_specs = (P("blk", None), P("rep", "blk"))
    out_specs = (P("rep", "blk"), P("rep", "blk"))
    return jax.shard_map(
        per_device, mesh=mesh, in_specs=in_specs, out_specs=out_specs, check_vma=False
    )
```

profile of v0, /device:TPU:0, one launch (start us, length us, event | category | flops | bytes accessed | tf_op | source)
XLA Modules:
  0.0 183.7 jit_solution(12723505699822419723)
XLA Ops:
  0.6 33.2 %all_gather.9 = bf16[1024,256]{1,0:T(8,128)(2,1)S(1)} all-gather(bf16[128,256]{1,0:T(8,128)(2,1)} %param.2), channel_id=1, replica_groups=mesh['blk'=8,'rep'=4] {'blk'}, dimensions={0}, use_global_device_ids=true | all-gather | bytes 589824 | tf_op jit(solution)/shard_map/all_gather | solution.py:34
  33.9 0.0 copy-start.1
  33.9 0.2 multiply_reduce_fusion
  34.1 0.6 copy-done.1
  34.7 0.1 multiply_reduce_fusion.1
  34.8 0.0 copy-start
  34.8 0.5 fusion.4
  35.3 0.3 copy-done
  35.6 30.5 %all_gather.10 = f32[32,1024]{1,0:T(8,128)S(1)} all-gather(f32[32,128]{1,0:T(8,128)S(1)} %copy-done), channel_id=1, replica_groups=mesh['blk'=8,'rep'=4] {'blk'}, dimensions={1}, use_global_device_ids=true | all-gather | bytes 147456 | tf_op jit(solution)/shard_map/all_gather | solution.py:38
  66.1 1.2 multiply_reduce_fusion.4
  67.3 40.0 %all-reduce.1 = (f32[]{:T(128)}, f32[]{:T(128)}) all-reduce(f32[]{:T(128)} %get-tuple-element.5, f32[]{:T(128)} %get-tuple-element.4), channel_id=1, replica_groups=mesh['blk'=8,'rep'=4] {'blk','rep'}, use_global_device_ids=true, to_apply=%region_1.0 | all-reduce | flops 2 | bytes 16 | tf_op jit(solution)/shard_map/psum | solution.py:26
  108.6 30.5 %all_gather.11 = f32[32,1024]{1,0:T(8,128)S(1)} all-gather(f32[32,128]{1,0:T(8,128)S(1)} %multiply_subtract_fusion.1), channel_id=1, replica_groups=mesh['blk'=8,'rep'=4] {'blk'}, dimensions={1}, use_global_device_ids=true | all-gather | bytes 147456 | tf_op jit(solution)/shard_map/all_gather | solution.py:38
  139.1 1.3 multiply_reduce_fusion.2
  140.4 38.1 %all-reduce = (f32[]{:T(128)}, f32[]{:T(128)}) all-reduce(f32[]{:T(128)} %get-tuple-element.3, f32[]{:T(128)} %get-tuple-element.2), channel_id=1, replica_groups=mesh['blk'=8,'rep'=4] {'blk','rep'}, use_global_device_ids=true, to_apply=%region_7.8 | all-reduce | flops 2 | bytes 16 | tf_op jit(solution)/shard_map/psum | solution.py:26
  183.1 0.6 multiply_subtract_fusion
  (2 shorter events, 0.0 us)
Async XLA Ops:
  33.9 0.8 copy-start.1
  34.8 0.7 copy-start
where the time goes:
time: 185 us; the launch traced here: 184 us
  blocking collectives  172 us (93%)
  between operations  6.59 us (4%)
  matrix products  2.96 us (2%)
    psum x2, blocking collectives, paired(): lax.psum((jnp.sum(residual * residual), jnp.sum(residual * image)), ('blk...  78.1 us
    all_gather x2, blocking collectives, folded_image(): piece = lax.all_gather(direction, 'blk', axis=1, tiled=True)  61 us
    all_gather x1, blocking collectives, per_device(): everyone = lax.all_gather(embeddings, 'blk', axis=0, tiled=True)  33.2 us

commit v1 on v0

--- a/solution.py
+++ b/solution.py
@@ -1,13 +1,329 @@
+import functools
+
 import jax
 import jax.numpy as jnp
 from jax import lax
+from jax.experimental import pallas as pl
+from jax.experimental.pallas import tpu as pltpu
 from jax.sharding import PartitionSpec as P
 
 ITERS = 2
-
+MESH = pl.DeviceIdType.MESH
+TINY = 1e-30
 
 length_scale = 1.0
 noise_var = 1.0
+
+
+def flip(index, mask):
+    bit = 1
+    while bit <= mask:
+        if mask & bit:
+            index = index + bit * (1 - 2 * ((index // bit) % 2))
+        bit *= 2
+    return index
+
+
+def dot_nt(a, b):
+    return lax.dot_general(a, b, (((1,), (1,)), ((), ())), preferred_element_type=jnp.float32)
+
+
+def split(x):
+    high = x.astype(jnp.bfloat16)
+    low = (x - high.astype(jnp.float32)).astype(jnp.bfloat16)
+    return high, low
+
+
+def product(v_ref, high_ref, low_ref, rhs, rows, columns):
+    both = jnp.dot(v_ref[:, rows], high_ref[rows, columns], preferred_element_type=jnp.float32)
+    low = jnp.dot(v_ref[pl.ds(0, rhs), rows], low_ref[rows, columns], preferred_element_type=jnp.float32)
+    return both[:rhs] + (both[rhs:] + low)
+
+
+def fold(x):
+    rows = jnp.sum(x, axis=0, keepdims=True)
+    total = rows[:, :128]
+    for at in range(128, rows.shape[1], 128):
+        total = total + rows[:, at : at + 128]
+    return total
+
+
+def kernel(
+    n_blk,
+    n_rep,
+    emb_hbm,
+    tgt_hbm,
+    out_ref,
+    emb,
+    tgt,
+    scaled,
+    col_norm,
+    row_norm,
+    k_high,
+    k_low,
+    v_pair,
+    image,
+    parts,
+    load_sem,
+    emb_send,
+    emb_recv,
+    tgt_send,
+    tgt_recv,
+    core_send,
+    core_recv,
+    part_send,
+    part_recv,
+):
+    pts, dim = emb.shape[2] * 2, emb.shape[3]
+    rhs = tgt.shape[1]
+    me = lax.axis_index("blk")
+    rep = lax.axis_index("rep")
+    half = rep % 2
+    masks = [0, 1] + list(range(2, n_blk, 2)) + list(range(3, n_blk, 2))
+    place = {mask: p for p, mask in enumerate(masks)}
+    direct = [1] + list(range(2, n_blk, 2))
+
+    loads = [
+        pltpu.make_async_copy(emb_hbm.at[pl.ds(i * (pts // 2), pts // 2)], emb.at[0, i], load_sem.at[i])
+        for i in range(2)
+    ] + [pltpu.make_async_copy(tgt_hbm, tgt.at[0], load_sem.at[2])]
+    for load in loads:
+        load.start()
+
+    barrier = pltpu.get_barrier_semaphore()
+    for mask in direct:
+        pl.semaphore_signal(barrier, inc=1, device_id=(flip(me, mask), rep), device_id_type=MESH)
+    for mask in range(1, n_rep):
+        pl.semaphore_signal(barrier, inc=1, device_id=(me, flip(rep, mask)), device_id_type=MESH)
+    for load in loads:
+        load.wait()
+    pl.semaphore_wait(barrier, len(direct) + n_rep - 1)
+
+    def send_emb(source, target, to):
+        return pltpu.make_async_remote_copy(
+            src_ref=emb.at[source, half],
+            dst_ref=emb.at[target, half],
+            send_sem=emb_send.at[target],
+            recv_sem=emb_recv.at[target],
+            device_id=(flip(me, to), rep),
+            device_id_type=MESH,
+        )
+
+    def send_tgt(source, target, to):
+        return pltpu.make_async_remote_copy(
+            src_ref=tgt.at[source],
+            dst_ref=tgt.at[target],
+            send_sem=tgt_send.at[target],
+            recv_sem=tgt_recv.at[target],
+            device_id=(flip(me, to), rep),
+            device_id_type=MESH,
+        )
+
+    def send_core(at):
+        return pltpu.make_async_remote_copy(
+            src_ref=emb.at[at, half],
+            dst_ref=emb.at[at, half],
+            send_sem=core_send.at[at],
+            recv_sem=core_recv.at[at],
+            device_id=(me, flip(rep, 1)),
+            device_id_type=MESH,
+        )
+
+    emb_copies, tgt_copies, core_copies = {}, {}, {}
+    for mask in sorted(direct, reverse=True):
+        p = place[mask]
+        emb_copies[p] = send_emb(0, p, mask)
+        emb_copies[p].start()
+    for mask in sorted(direct, reverse=True):
+        p = place[mask]
+        tgt_copies[p] = send_tgt(0, p, mask)
+        tgt_copies[p].start()
+
+    def arrive(p):
+        mask = masks[p]
+        onward = place[mask + 1] if mask >= 2 and mask % 2 == 0 else None
+        if onward is not None:
+            emb_copies[onward] = send_emb(p, onward, 1)
+            tgt_copies[onward] = send_tgt(p, onward, 1)
+        emb_copies[p].wait_recv()
+        core_copies[p] = send_core(p)
+        core_copies[p].start()
+        if onward is not None:
+            emb_copies[onward].start()
+        tgt_copies[p].wait_recv()
+        if onward is not None:
+            tgt_copies[onward].start()
+
+    def tile(own, own_norm, far, far_norm):
+        distance = jnp.maximum((own_norm + far_norm) + dot_nt(own, far), TINY)
+        return jnp.exp(-(distance * lax.rsqrt(distance)) / length_scale)
+
+    ones = jnp.ones((8, dim), jnp.bfloat16)
+
+    def build(p):
+        here = pl.ds(p * pts, pts)
+        points = emb[p].reshape(pts, dim)
+        wide = points.astype(jnp.float32)
+        squares = wide * wide
+        col_norm[here, :] = jnp.sum(squares, axis=1, keepdims=True)
+        s_high, s_low = split(squares)
+        row_norm[:, here] = dot_nt(ones, s_high) + dot_nt(ones, s_low)
+        scaled[here, :] = -2.0 * points
+        v_high, v_low = split(tgt[p])
+        v_pair[pl.ds(0, rhs), here] = v_high
+        v_pair[pl.ds(rhs, rhs), here] = v_low
+        upto, before = pl.ds(0, (p + 1) * pts), pl.ds(0, p * pts)
+        far = emb[0 : p + 1].reshape((p + 1) * pts, dim)
+        for_row = tile(scaled[here, :], col_norm[here, :], far, row_norm[0:1, upto])
+        diagonal = for_row[:, p * pts :]
+        row_id = lax.broadcasted_iota(jnp.int32, (pts, pts), 0)
+        col_id = lax.broadcasted_iota(jnp.int32, (pts, pts), 1)
+        d_high, d_low = split(jnp.where(row_id == col_id, 1.0, diagonal))
+        k_high[here, here] = d_high
+        k_low[here, here] = d_low
+        if p:
+            r_high, r_low = split(for_row[:, : p * pts])
+            k_high[here, before] = r_high
+            k_low[here, before] = r_low
+            for_col = tile(scaled[before, :], col_norm[before, :], points, row_norm[0:1, here])
+            c_high, c_low = split(for_col)
+            k_high[before, here] = c_high
+            k_low[before, here] = c_low
+            image[:, before] += product(v_pair, k_high, k_low, rhs, here, before)
+        image[:, here] = product(v_pair, k_high, k_low, rhs, upto, here)
+
+    build(0)
+    last_direct = len(direct)
+    for p in range(1, n_blk):
+        arrive(p)
+        core_copies[p].wait_recv()
+        build(p)
+
+    everything = jnp.concatenate([tgt[p] for p in range(n_blk)], axis=1)
+    along = image[...] + noise_var * everything
+    rr, pr = fold(everything * everything), fold(everything * along)
+    rr_sum = jnp.sum(rr, axis=1, keepdims=True)
+    pr_sum = jnp.sum(pr, axis=1, keepdims=True)
+
+    def step_of(norm, prod):
+        usable = jnp.logical_and(norm > 0.0, prod > 0.0)
+        return jnp.where(usable, norm / jnp.where(usable, prod, 1.0), 1.0)
+
+    local = step_of(rr_sum, pr_sum)
+    w = everything - local * along
+    w_high, w_low = split(w)
+    v_pair[pl.ds(0, rhs), :] = w_high
+    v_pair[pl.ds(rhs, rhs), :] = w_low
+    whole = pl.ds(0, n_blk * pts)
+    aw = product(v_pair, k_high, k_low, rhs, whole, whole) + noise_var * w
+    aa = (along - aw) / local
+    sums = jnp.concatenate(
+        [
+            rr,
+            pr,
+            fold(w * w),
+            fold(w * along),
+            fold(along * along),
+            fold(w * aw),
+            fold(w * aa + along * aw),
+            fold(along * aa),
+        ],
+        axis=0,
+    )
+    parts[0] = jnp.broadcast_to(jnp.sum(sums, axis=1, keepdims=True), parts.shape[1:])
+    part_copies = []
+    for mask in range(1, n_rep):
+        copy = pltpu.make_async_remote_copy(
+            src_ref=parts.at[0],
+            dst_ref=parts.at[mask],
+            send_sem=part_send.at[mask],
+            recv_sem=part_recv.at[mask],
+            device_id=(me, flip(rep, mask)),
+            device_id_type=MESH,
+        )
+        copy.start()
+        part_copies.append(copy)
+    for p in range(1, n_blk):
+        emb_copies[p].wait_send()
+        tgt_copies[p].wait_send()
+        core_copies[p].wait_send()
+    for copy in part_copies:
+        copy.wait()
+
+    tiles = [parts[i] for i in range(n_rep)]
+    norm_now = sum(t[0:1] for t in tiles)
+    alpha = norm_now / sum(t[1:2] for t in tiles)
+    norm_next = jnp.zeros_like(norm_now)
+    prod = jnp.zeros_like(norm_now)
+    for t in tiles:
+        delta = alpha - step_of(t[0:1], t[1:2])
+        norm_next = norm_next + (t[2:3] - delta * (2.0 * t[3:4] - delta * t[4:5]))
+        prod = prod + (t[5:6] - delta * (t[6:7] - delta * t[7:8]))
+    ratio = norm_next / norm_now
+    alpha_next = norm_next / (prod - ratio * norm_next / alpha)
+    delta = alpha - step_of(tiles[0][0:1], tiles[0][1:2])
+    own_t, own_a = everything[:, :pts], along[:, :pts]
+    residual = w[:, :pts] - delta * own_a
+    image_r = aw[:, :pts] - delta * aa[:, :pts]
+    direction = residual + ratio * own_t
+    out_ref[0] = alpha * own_t + alpha_next * direction
+    out_ref[1] = residual - alpha_next * (image_r + ratio * own_a)
+
+
+def fused(n_blk, n_rep, embeddings, targets):
+    pts, dim = embeddings.shape
+    rhs = targets.shape[0]
+    total = n_blk * pts
+    dma = pltpu.SemaphoreType.DMA
+    out = pl.pallas_call(
+        functools.partial(kernel, n_blk, n_rep),
+        out_shape=jax.ShapeDtypeStruct((2, rhs, pts), jnp.float32),
+        in_specs=[pl.BlockSpec(memory_space=pl.ANY)] * 2,
+        out_specs=pl.BlockSpec(memory_space=pltpu.VMEM),
+        scratch_shapes=[
+            pltpu.VMEM((n_blk, 2, pts // 2, dim), jnp.bfloat16),
+            pltpu.VMEM((n_blk, rhs, pts), jnp.float32),
+            pltpu.VMEM((total, dim), jnp.bfloat16),
+            pltpu.VMEM((total, 1), jnp.float32),
+            pltpu.VMEM((8, total), jnp.float32),
+            pltpu.VMEM((total, total), jnp.bfloat16),
+            pltpu.VMEM((total, total), jnp.bfloat16),
+            pltpu.VMEM((2 * rhs, total), jnp.bfloat16),
+            pltpu.VMEM((rhs, total), jnp.float32),
+            pltpu.VMEM((n_rep, 8, 128), jnp.float32),
+            dma((3,)),
+            dma((n_blk,)),
+            dma((n_blk,)),
+            dma((n_blk,)),
+            dma((n_blk,)),
+            dma((n_blk,)),
+            dma((n_blk,)),
+            dma((n_rep,)),
+            dma((n_rep,)),
+        ],
+        compiler_params=pltpu.CompilerParams(collective_id=0, has_side_effects=True),
+    )(embeddings, targets)
+    return out[0], out[1]
+
+
+def power_of_two(n):
+    return n >= 2 and n & (n - 1) == 0
+
+
+def fits(n_blk, n_rep, embeddings, targets):
+    pts, dim = embeddings.shape
+    rhs = targets.shape[0]
+    total = n_blk * pts
+    return (
+        power_of_two(n_blk)
+        and power_of_two(n_rep)
+        and pts == 128
+        and dim % 128 == 0
+        and rhs % 16 == 0
+        and rhs <= 128
+        and total <= 2048
+        and dim <= 1024
+    )
 
 
 def squared_norms(points):
@@ -70,8 +386,13 @@
 
 
 def solution(mesh):
+    n_blk, n_rep = mesh.shape["blk"], mesh.shape["rep"]
+
+    def step(embeddings, targets):
+        if fits(n_blk, n_rep, embeddings, targets):
+            return fused(n_blk, n_rep, embeddings, targets)
+        return per_device(embeddings, targets)
+
     in_specs = (P("blk", None), P("rep", "blk"))
     out_specs = (P("rep", "blk"), P("rep", "blk"))
-    return jax.shard_map(
-        per_device, mesh=mesh, in_specs=in_specs, out_specs=out_specs, check_vma=False
-    )
+    return jax.shard_map(step, mesh=mesh, in_specs=in_specs, out_specs=out_specs, check_vma=False)

time: 185 us -> 27.4 us (0.15)
  blocking collectives: 172 us -> 0 us
  Pallas kernels: 0 us -> 25.1 us
  between operations: 6.59 us -> 0.64 us
  matrix products: 2.96 us -> 0 us
    all_gather x3 -> x0, blocking collectives: 94.3 us -> none  [the longest x2 61 us: folded_image(): piece = lax.all_gather(direction, 'blk', axis=1, tiled=True)]
    psum x2 -> x0, blocking collectives: 78.1 us -> none  [paired(): lax.psum((jnp.sum(residual * residual), jnp.sum(residual * image)), ('blk...]
    pallas_call x0 -> x1, Pallas kernels: none -> 25.1 us  [fused(): pl.pallas_call(functools.partial(kernel, n_blk, n_rep), out_shape=jax.Sha...]
    dot_general x3 -> x0, matrix products: 2.96 us -> none  [the longest x2 2.51 us: folded_image(): jnp.einsum('rq,pq->rp', piece, tile, precision=lax.Precision.HIGHEST, pre...]
where the time goes in v1:
time: 27.4 us; the launch traced here: 27.1 us
  Pallas kernels  25.1 us (92%)
  local copies, waits for them, and re-layouts  1.35 us (5%)
  between operations  0.64 us (2%)
    pallas_call x1, Pallas kernels, fused(): pl.pallas_call(functools.partial(kernel, n_blk, n_rep), out_shape=jax.Sha...  25.1 us
    squeeze x1, local copies, waits for them, and re-layouts, fused(): return (out[0], out[1])  1.35 us

profile of v1, /device:TPU:0, one launch (start us, length us, event | category | flops | bytes accessed | tf_op | source)
XLA Modules:
  0.0 27.1 jit_solution(12672690612624502465)
XLA Ops:
  0.6 25.1 %shard_map.41 = f32[2,32,128]{2,1,0:T(8,128)} custom-call(bf16[128,256]{1,0:T(8,128)(2,1)} %emb_hbm.1, f32[32,128]{1,0:T(8,128)} %tgt_hbm.1), custom_call_target="tpu_custom_call" | custom-call | tf_op jit(solution)/shard_map/pallas_call | solution.py:278
  25.8 1.3 %slice_bitcast_fusion = (f32[32,128]{1,0:T(8,128)}, f32[32,128]{1,0:T(8,128)}) fusion(f32[2,32,128]{2,1,0:T(8,128)} %shard_map.41), kind=kLoop, calls=%fused_computation | loop fusion | bytes 65536 | tf_op jit(solution)/shard_map/squeeze | solution.py:306

commit v2 on v1

--- a/solution.py
+++ b/solution.py
@@ -62,7 +62,6 @@
     k_high,
     k_low,
     v_pair,
-    image,
     parts,
     load_sem,
     emb_send,
@@ -139,19 +138,20 @@
         tgt_copies[p] = send_tgt(0, p, mask)
         tgt_copies[p].start()
 
-    def arrive(p):
-        mask = masks[p]
-        onward = place[mask + 1] if mask >= 2 and mask % 2 == 0 else None
-        if onward is not None:
-            emb_copies[onward] = send_emb(p, onward, 1)
-            tgt_copies[onward] = send_tgt(p, onward, 1)
+    def take_emb(p):
+        onward = place[masks[p] + 1] if masks[p] in direct[1:] else None
         emb_copies[p].wait_recv()
         core_copies[p] = send_core(p)
         core_copies[p].start()
         if onward is not None:
+            emb_copies[onward] = send_emb(p, onward, 1)
             emb_copies[onward].start()
+
+    def take_tgt(p):
+        onward = place[masks[p] + 1] if masks[p] in direct[1:] else None
         tgt_copies[p].wait_recv()
         if onward is not None:
+            tgt_copies[onward] = send_tgt(p, onward, 1)
             tgt_copies[onward].start()
 
     def tile(own, own_norm, far, far_norm):
@@ -169,9 +169,6 @@
         s_high, s_low = split(squares)
         row_norm[:, here] = dot_nt(ones, s_high) + dot_nt(ones, s_low)
         scaled[here, :] = -2.0 * points
-        v_high, v_low = split(tgt[p])
-        v_pair[pl.ds(0, rhs), here] = v_high
-        v_pair[pl.ds(rhs, rhs), here] = v_low
         upto, before = pl.ds(0, (p + 1) * pts), pl.ds(0, p * pts)
         far = emb[0 : p + 1].reshape((p + 1) * pts, dim)
         for_row = tile(scaled[here, :], col_norm[here, :], far, row_norm[0:1, upto])
@@ -189,18 +186,40 @@
             c_high, c_low = split(for_col)
             k_high[before, here] = c_high
             k_low[before, here] = c_low
-            image[:, before] += product(v_pair, k_high, k_low, rhs, here, before)
-        image[:, here] = product(v_pair, k_high, k_low, rhs, upto, here)
 
     build(0)
-    last_direct = len(direct)
-    for p in range(1, n_blk):
-        arrive(p)
+    n_direct = len(direct)
+
+    def add(p):
         core_copies[p].wait_recv()
         build(p)
 
+    for p in range(1, n_direct + 1):
+        take_emb(p)
+    for p in range(1, n_direct):
+        add(p)
+    for p in range(1, n_direct + 1):
+        take_tgt(p)
+    if n_direct + 1 < n_blk:
+        take_emb(n_direct + 1)
+    add(n_direct)
+    for p in range(n_direct + 2, n_blk):
+        take_emb(p)
+    for p in range(n_direct + 1, n_blk):
+        add(p)
+    for p in range(n_direct + 1, n_blk):
+        take_tgt(p)
+
+    whole = pl.ds(0, n_blk * pts)
+
+    def apply(v):
+        v_high, v_low = split(v)
+        v_pair[pl.ds(0, rhs), :] = v_high
+        v_pair[pl.ds(rhs, rhs), :] = v_low
+        return product(v_pair, k_high, k_low, rhs, whole, whole) + noise_var * v
+
     everything = jnp.concatenate([tgt[p] for p in range(n_blk)], axis=1)
-    along = image[...] + noise_var * everything
+    along = apply(everything)
     rr, pr = fold(everything * everything), fold(everything * along)
     rr_sum = jnp.sum(rr, axis=1, keepdims=True)
     pr_sum = jnp.sum(pr, axis=1, keepdims=True)
@@ -211,11 +230,7 @@
 
     local = step_of(rr_sum, pr_sum)
     w = everything - local * along
-    w_high, w_low = split(w)
-    v_pair[pl.ds(0, rhs), :] = w_high
-    v_pair[pl.ds(rhs, rhs), :] = w_low
-    whole = pl.ds(0, n_blk * pts)
-    aw = product(v_pair, k_high, k_low, rhs, whole, whole) + noise_var * w
+    aw = apply(w)
     aa = (along - aw) / local
     sums = jnp.concatenate(
         [
@@ -289,7 +304,6 @@
             pltpu.VMEM((total, total), jnp.bfloat16),
             pltpu.VMEM((total, total), jnp.bfloat16),
             pltpu.VMEM((2 * rhs, total), jnp.bfloat16),
-            pltpu.VMEM((rhs, total), jnp.float32),
             pltpu.VMEM((n_rep, 8, 128), jnp.float32),
             dma((3,)),
             dma((n_blk,)),

time: 27.4 us -> 24.3 us (0.89)
  Pallas kernels: 25.1 us -> 22 us
    pallas_call x1, Pallas kernels: 25.1 us -> 22 us  [fused(): pl.pallas_call(functools.partial(kernel, n_blk, n_rep), out_shape=jax.Sha...]
where the time goes in v2:
time: 24.3 us; the launch traced here: 24 us
  Pallas kernels  22 us (91%)
  local copies, waits for them, and re-layouts  1.35 us (6%)
  between operations  0.64 us (3%)
    pallas_call x1, Pallas kernels, fused(): pl.pallas_call(functools.partial(kernel, n_blk, n_rep), out_shape=jax.Sha...  22 us
    squeeze x1, local copies, waits for them, and re-layouts, fused(): return (out[0], out[1])  1.35 us

profile of v2, /device:TPU:0, one launch (start us, length us, event | category | flops | bytes accessed | tf_op | source)
XLA Modules:
  0.0 24.0 jit_solution(18086481746060229939)
XLA Ops:
  0.6 22.0 %shard_map.41 = f32[2,32,128]{2,1,0:T(8,128)} custom-call(bf16[128,256]{1,0:T(8,128)(2,1)} %emb_hbm.1, f32[32,128]{1,0:T(8,128)} %tgt_hbm.1), custom_call_target="tpu_custom_call" | custom-call | tf_op jit(solution)/shard_map/pallas_call | solution.py:293
  22.6 1.3 %slice_bitcast_fusion = (f32[32,128]{1,0:T(8,128)}, f32[32,128]{1,0:T(8,128)}) fusion(f32[2,32,128]{2,1,0:T(8,128)} %shard_map.41), kind=kLoop, calls=%fused_computation | loop fusion | bytes 65536 | tf_op jit(solution)/shard_map/squeeze | solution.py:320

commit v3 on v2

--- a/solution.py
+++ b/solution.py
@@ -129,11 +129,11 @@
         )
 
     emb_copies, tgt_copies, core_copies = {}, {}, {}
-    for mask in sorted(direct, reverse=True):
+    for mask in direct:
         p = place[mask]
         emb_copies[p] = send_emb(0, p, mask)
         emb_copies[p].start()
-    for mask in sorted(direct, reverse=True):
+    for mask in direct:
         p = place[mask]
         tgt_copies[p] = send_tgt(0, p, mask)
         tgt_copies[p].start()
@@ -141,11 +141,11 @@
     def take_emb(p):
         onward = place[masks[p] + 1] if masks[p] in direct[1:] else None
         emb_copies[p].wait_recv()
-        core_copies[p] = send_core(p)
-        core_copies[p].start()
         if onward is not None:
             emb_copies[onward] = send_emb(p, onward, 1)
             emb_copies[onward].start()
+        core_copies[p] = send_core(p)
+        core_copies[p].start()
 
     def take_tgt(p):
         onward = place[masks[p] + 1] if masks[p] in direct[1:] else None
@@ -182,10 +182,8 @@
             r_high, r_low = split(for_row[:, : p * pts])
             k_high[here, before] = r_high
             k_low[here, before] = r_low
-            for_col = tile(scaled[before, :], col_norm[before, :], points, row_norm[0:1, here])
-            c_high, c_low = split(for_col)
-            k_high[before, here] = c_high
-            k_low[before, here] = c_low
+            k_high[before, here] = r_high.T
+            k_low[before, here] = r_low.T
 
     build(0)
     n_direct = len(direct)
@@ -196,10 +194,11 @@
 
     for p in range(1, n_direct + 1):
         take_emb(p)
-    for p in range(1, n_direct):
-        add(p)
+    add(1)
     for p in range(1, n_direct + 1):
         take_tgt(p)
+    for p in range(2, n_direct):
+        add(p)
     if n_direct + 1 < n_blk:
         take_emb(n_direct + 1)
     add(n_direct)

time: 24.3 us -> 22.7 us (0.934)
  Pallas kernels: 22 us -> 20.4 us
    pallas_call x1, Pallas kernels: 22 us -> 20.4 us  [fused(): pl.pallas_call(functools.partial(kernel, n_blk, n_rep), out_shape=jax.Sha...]
where the time goes in v3:
time: 22.7 us; the launch traced here: 22.4 us
  Pallas kernels  20.4 us (90%)
  local copies, waits for them, and re-layouts  1.35 us (6%)
  between operations  0.64 us (3%)
    pallas_call x1, Pallas kernels, fused(): pl.pallas_call(functools.partial(kernel, n_blk, n_rep), out_shape=jax.Sha...  20.4 us
    squeeze x1, local copies, waits for them, and re-layouts, fused(): return (out[0], out[1])  1.35 us

profile of v3, /device:TPU:0, one launch (start us, length us, event | category | flops | bytes accessed | tf_op | source)
XLA Modules:
  0.0 22.4 jit_solution(2953778979871003195)
XLA Ops:
  0.6 20.4 %shard_map.41 = f32[2,32,128]{2,1,0:T(8,128)} custom-call(bf16[128,256]{1,0:T(8,128)(2,1)} %emb_hbm.1, f32[32,128]{1,0:T(8,128)} %tgt_hbm.1), custom_call_target="tpu_custom_call" | custom-call | tf_op jit(solution)/shard_map/pallas_call | solution.py:292
  21.1 1.3 %slice_bitcast_fusion = (f32[32,128]{1,0:T(8,128)}, f32[32,128]{1,0:T(8,128)}) fusion(f32[2,32,128]{2,1,0:T(8,128)} %shard_map.41), kind=kLoop, calls=%fused_computation | loop fusion | bytes 65536 | tf_op jit(solution)/shard_map/squeeze | solution.py:319

commit v4 on v3

--- a/solution.py
+++ b/solution.py
@@ -204,8 +204,8 @@
     add(n_direct)
     for p in range(n_direct + 2, n_blk):
         take_emb(p)
-    for p in range(n_direct + 1, n_blk):
-        add(p)
+        add(p - 1)
+    add(n_blk - 1)
     for p in range(n_direct + 1, n_blk):
         take_tgt(p)
 

time: 22.7 us -> 22.4 us (0.987)
  Pallas kernels: 20.4 us -> 20.1 us
    pallas_call x1, Pallas kernels: 20.4 us -> 20.1 us  [fused(): pl.pallas_call(functools.partial(kernel, n_blk, n_rep), out_shape=jax.Sha...]
where the time goes in v4:
time: 22.4 us; the launch traced here: 22.1 us
  Pallas kernels  20.1 us (90%)
  local copies, waits for them, and re-layouts  1.35 us (6%)
  between operations  0.64 us (3%)
    pallas_call x1, Pallas kernels, fused(): pl.pallas_call(functools.partial(kernel, n_blk, n_rep), out_shape=jax.Sha...  20.1 us
    squeeze x1, local copies, waits for them, and re-layouts, fused(): return (out[0], out[1])  1.35 us

profile of v4, /device:TPU:0, one launch (start us, length us, event | category | flops | bytes accessed | tf_op | source)
XLA Modules:
  0.0 22.1 jit_solution(9835740076837331837)
XLA Ops:
  0.6 20.1 %shard_map.41 = f32[2,32,128]{2,1,0:T(8,128)} custom-call(bf16[128,256]{1,0:T(8,128)(2,1)} %emb_hbm.1, f32[32,128]{1,0:T(8,128)} %tgt_hbm.1), custom_call_target="tpu_custom_call" | custom-call | tf_op jit(solution)/shard_map/pallas_call | solution.py:292
  20.8 1.3 %slice_bitcast_fusion = (f32[32,128]{1,0:T(8,128)}, f32[32,128]{1,0:T(8,128)}) fusion(f32[2,32,128]{2,1,0:T(8,128)} %shard_map.41), kind=kLoop, calls=%fused_computation | loop fusion | bytes 65536 | tf_op jit(solution)/shard_map/squeeze | solution.py:319
